TPU v7x, 32 devices: a whole 2x2x4 slice. The times are simulated.
32 devices in a mesh: scan: 8 (over z, x), tile: 4 (over y, core).
Axes of the slice: x: 2, y: 2, z: 4, core: 2. Of those that a mesh axis runs over, the one named last changes fastest.
Arguments:
- object_slab: float32 [2, 3072, 6144], P(None, 'tile', 'scan'), may hold values from -6 to 6
- probe_field: float32 [2, 512, 512], replicated, may hold values from -3 to 3
- intensities: bfloat16 [8, 4, 6, 512, 512], P('scan', 'tile'), may hold values from 0 to 2
- offsets: int32 [8, 4, 6, 2], P('scan', 'tile'), may hold values from 0 to 767
- live_count: int32 [8, 4], P(None, 'tile'), may hold values from 1 to 6, as said below
Outputs:
- object_grad: float32 [2, 3072, 6144], P(None, 'tile', 'scan')
Inputs may be any that keep to these rules, and one draw needn't show every extreme that they name: The first live_count slots of a group hold its measured positions; some group has all 6 slots live.
All inputs are finite; a program needn't handle non-finite values.
Results may differ from a plain program's by a relative error of at most 0.014.
Values may be sent and summed in bfloat16 or wider, within the bound.
A program may use at most 128 MiB of HBM per device.

v0:
```python
import functools
import math

import jax
import jax.numpy as jnp
import numpy as np
from jax import lax
from jax.experimental import pallas as pl
from jax.experimental.pallas import tpu as pltpu
from jax.sharding import PartitionSpec as P

RADIX = 4
LANES = 128
vmem_bytes = 67043328


def residue_tables(side_len):
    part = side_len // RADIX
    freq = np.arange(side_len).reshape(part, RADIX).T
    across = np.arange(part)
    phase = (freq[:, :, None] * across[None, None, :] % side_len) * (2.0 * math.pi / side_len)
    factor = 1.0 / math.sqrt(side_len)
    cos = np.cos(phase) * factor
    sin = np.sin(phase) * factor
    rows = np.concatenate(
        [np.concatenate([cos, sin], axis=2), np.concatenate([-sin, cos], axis=2)], axis=1
    ).astype(np.float32)
    return jnp.asarray(rows, jnp.bfloat16), jnp.asarray(rows.swapaxes(1, 2), jnp.bfloat16)


def sorted_by_residue(side_len):
    at = np.arange(side_len)
    source = at % (side_len // RADIX) * RADIX + at // (side_len // RADIX)
    sort = (source[:, None] == at[None, :]).astype(np.float32)
    return jnp.asarray(sort, jnp.bfloat16), jnp.asarray(sort.T, jnp.bfloat16)


def dot(a, b):
    return jnp.dot(a, b, preferred_element_type=jnp.float32)


def butterfly(parts, sign):
    (r0, i0), (r1, i1), (r2, i2), (r3, i3) = parts
    ar, ai, br, bi = r0 + r2, i0 + i2, r1 + r3, i1 + i3
    cr, ci, dr, di = r0 - r2, i0 - i2, r1 - r3, i1 - i3
    plus = (cr - di, ci + dr)
    minus = (cr + di, ci - dr)
    first, third = (plus, minus) if sign > 0 else (minus, plus)
    return [(ar + br, ai + bi), first, (ar - br, ai - bi), third]


def neighbours(axes):
    result = []
    for name, count in axes:
        me = lax.axis_index(name)
        result.append((me > 0, {name: me - 1}, me < count - 1, {name: me + 1}))
    return result


def meet(peers):
    barrier = pltpu.get_barrier_semaphore()
    for has_low, low, has_high, high in peers:
        for there, peer in ((has_low, low), (has_high, high)):

            @pl.when(there)
            def _(peer=peer):
                pl.semaphore_signal(
                    barrier, inc=1, device_id=peer, device_id_type=pl.DeviceIdType.MESH
                )

    count = sum(
        there.astype(jnp.int32) for has_low, _, has_high, _ in peers for there in (has_low, has_high)
    )
    pl.semaphore_wait(barrier, count)


def remote(source, target, sends, receives, index, peer):
    return pltpu.make_async_remote_copy(
        src_ref=source,
        dst_ref=target,
        send_sem=sends.at[index],
        recv_sem=receives.at[index],
        device_id=peer,
        device_id_type=pl.DeviceIdType.MESH,
    )


def gather_kernel(
    axes,
    own_hbm,
    measured_hbm,
    sort_hbm,
    unsort_hbm,
    right_hbm,
    below_hbm,
    corner_hbm,
    sorted_hbm,
    own,
    sent,
    right,
    below,
    corner,
    measured,
    arranged,
    sort,
    unsort,
    sends,
    receives,
    fetches,
    puts,
):
    side_len = measured.shape[-1]
    scan, tile = neighbours(axes)
    has_left, left, has_right, _ = scan
    has_up, up, has_down, _ = tile
    first = pltpu.make_async_copy(
        own_hbm.at[:, :side_len, :side_len], own.at[:, :side_len, :side_len], fetches.at[0]
    )
    second = pltpu.make_async_copy(
        own_hbm.at[:, side_len:, :side_len], own.at[:, side_len:, :side_len], fetches.at[1]
    )
    third = pltpu.make_async_copy(
        own_hbm.at[:, :side_len, side_len:], own.at[:, :side_len, side_len:], fetches.at[2]
    )
    fetch_measured = pltpu.make_async_copy(measured_hbm, measured, fetches.at[3])
    fetch_sort = pltpu.make_async_copy(sort_hbm, sort, fetches.at[4])
    fetch_unsort = pltpu.make_async_copy(unsort_hbm, unsort, fetches.at[5])
    first.start()
    second.start()
    third.start()
    fetch_sort.start()
    fetch_unsort.start()
    fetch_measured.start()
    top = remote(
        sent.at[:, :side_len, :side_len], right.at[:, :side_len, :], sends, receives, 0, left
    )
    rest = remote(
        sent.at[:, side_len:, :side_len], right.at[:, side_len:, :], sends, receives, 1, left
    )
    under = remote(sent.at[:, :side_len, :], below, sends, receives, 2, up)
    across = remote(right.at[:, :side_len, :], corner, sends, receives, 3, up)
    first.wait()
    sent[:, :side_len, :side_len] = own[:, :side_len, :side_len].astype(jnp.bfloat16)
    meet((scan, tile))

    @pl.when(has_left)
    def _():
        top.start()

    second.wait()
    third.wait()
    sent[:, side_len:, :side_len] = own[:, side_len:, :side_len].astype(jnp.bfloat16)
    sent[:, :side_len, side_len:] = own[:, :side_len, side_len:].astype(jnp.bfloat16)

    @pl.when(has_left)
    def _():
        rest.start()

    @pl.when(has_up)
    def _():
        under.start()

    @pl.when(jnp.logical_not(has_right))
    def _():
        right[...] = jnp.zeros_like(right)

    @pl.when(jnp.logical_not(has_down))
    def _():
        below[...] = jnp.zeros_like(below)
        corner[...] = jnp.zeros_like(corner)

    fetch_sort.wait()
    fetch_unsort.wait()
    fetch_measured.wait()

    def sort_slot(slot, carry):
        rows = dot(sort[...], measured[slot]).astype(jnp.bfloat16)
        arranged[slot] = dot(rows, unsort[...]).astype(jnp.bfloat16)
        return carry

    lax.fori_loop(0, measured.shape[0], sort_slot, 0)
    put_sorted = pltpu.make_async_copy(arranged, sorted_hbm, puts.at[0])
    put_sorted.start()

    @pl.when(has_right)
    def _():
        top.wait_recv()

    @pl.when(has_up)
    def _():
        across.start()

    put_top = pltpu.make_async_copy(
        right.at[:, :side_len, :], right_hbm.at[:, :side_len, :], puts.at[1]
    )
    put_top.start()

    @pl.when(has_down)
    def _():
        under.wait_recv()

    put_below = pltpu.make_async_copy(below, below_hbm, puts.at[2])
    put_below.start()

    @pl.when(has_right)
    def _():
        rest.wait_recv()

    put_rest = pltpu.make_async_copy(
        right.at[:, side_len:, :], right_hbm.at[:, side_len:, :], puts.at[3]
    )
    put_rest.start()

    @pl.when(has_down)
    def _():
        across.wait_recv()

    put_corner = pltpu.make_async_copy(corner, corner_hbm, puts.at[4])
    put_corner.start()

    @pl.when(has_left)
    def _():
        top.wait_send()
        rest.wait_send()

    @pl.when(has_up)
    def _():
        under.wait_send()
        across.wait_send()

    put_sorted.wait()
    put_top.wait()
    put_below.wait()
    put_rest.wait()
    put_corner.wait()


def gather(axes, own, measured):
    side_len = measured.shape[-1]
    tile_len = own.shape[1]
    hbm = pl.BlockSpec(memory_space=pltpu.HBM)
    right = (2, tile_len, side_len)
    below = (2, side_len, tile_len)
    corner = (2, side_len, side_len)
    return pl.pallas_call(
        functools.partial(gather_kernel, axes),
        out_shape=[
            jax.ShapeDtypeStruct(shape, jnp.bfloat16)
            for shape in (right, below, corner, measured.shape)
        ],
        in_specs=[hbm] * 4,
        out_specs=[hbm] * 4,
        scratch_shapes=[
            pltpu.VMEM(own.shape, jnp.float32),
            pltpu.VMEM(own.shape, jnp.bfloat16),
            pltpu.VMEM(right, jnp.bfloat16),
            pltpu.VMEM(below, jnp.bfloat16),
            pltpu.VMEM(corner, jnp.bfloat16),
            pltpu.VMEM(measured.shape, jnp.bfloat16),
            pltpu.VMEM(measured.shape, jnp.bfloat16),
            pltpu.VMEM((side_len, side_len), jnp.bfloat16),
            pltpu.VMEM((side_len, side_len), jnp.bfloat16),
            pltpu.SemaphoreType.DMA((4,)),
            pltpu.SemaphoreType.DMA((4,)),
            pltpu.SemaphoreType.DMA((6,)),
            pltpu.SemaphoreType.DMA((5,)),
        ],
        compiler_params=pltpu.CompilerParams(
            collective_id=0, has_side_effects=True, vmem_limit_bytes=vmem_bytes
        ),
    )(own, measured, *sorted_by_residue(side_len))


def scatter_kernel(
    axes,
    own_hbm,
    spill_hbm,
    drop_hbm,
    both_hbm,
    total,
    spill,
    joined,
    landed,
    from_left,
    from_up,
    sends,
    receives,
    fetches,
):
    side_len = landed.shape[1]
    scan, tile = neighbours(axes)
    has_left, _, has_right, right = scan
    has_up, _, has_down, down = tile
    fetch_spill = pltpu.make_async_copy(spill_hbm.at[:, :side_len, :], spill, fetches.at[0])
    fetch_own = pltpu.make_async_copy(own_hbm, total, fetches.at[1])
    fetch_spill.start()
    fetch_own.start()
    meet((scan, tile))
    corner = remote(both_hbm, landed, sends, receives, 0, down)
    under = remote(drop_hbm, from_up, sends, receives, 1, down)
    rest = remote(
        spill_hbm.at[:, side_len:, :], from_left.at[:, side_len:, :], sends, receives, 2, right
    )
    top = remote(joined, from_left.at[:, :side_len, :], sends, receives, 3, right)

    @pl.when(has_down)
    def _():
        corner.start()

    @pl.when(has_right)
    def _():
        rest.start()

    @pl.when(has_down)
    def _():
        under.start()

    @pl.when(jnp.logical_not(has_up))
    def _():
        landed[...] = jnp.zeros_like(landed)

    fetch_spill.wait()

    @pl.when(has_up)
    def _():
        corner.wait_recv()

    joined[...] = (spill[...].astype(jnp.float32) + landed[...].astype(jnp.float32)).astype(
        jnp.bfloat16
    )

    @pl.when(has_right)
    def _():
        top.start()

    fetch_own.wait()

    @pl.when(has_left)
    def _():
        rest.wait_recv()
        total[:, side_len:, :side_len] += from_left[:, side_len:, :].astype(jnp.float32)

    @pl.when(has_up)
    def _():
        under.wait_recv()
        total[:, :side_len, :] += from_up[...].astype(jnp.float32)

    @pl.when(has_left)
    def _():
        top.wait_recv()
        total[:, :side_len, :side_len] += from_left[:, :side_len, :].astype(jnp.float32)

    @pl.when(has_right)
    def _():
        rest.wait_send()
        top.wait_send()

    @pl.when(has_down)
    def _():
        corner.wait_send()
        under.wait_send()


def scatter(axes, own, spill, dropped, both):
    hbm = pl.BlockSpec(memory_space=pltpu.HBM)
    return pl.pallas_call(
        functools.partial(scatter_kernel, axes),
        out_shape=pltpu.VMEM(own.shape, jnp.float32),
        in_specs=[hbm] * 4,
        out_specs=pl.BlockSpec(memory_space=pltpu.VMEM),
        scratch_shapes=[
            pltpu.VMEM(both.shape, jnp.bfloat16),
            pltpu.VMEM(both.shape, jnp.bfloat16),
            pltpu.VMEM(both.shape, jnp.bfloat16),
            pltpu.VMEM(spill.shape, jnp.bfloat16),
            pltpu.VMEM(dropped.shape, jnp.bfloat16),
            pltpu.SemaphoreType.DMA((4,)),
            pltpu.SemaphoreType.DMA((4,)),
            pltpu.SemaphoreType.DMA((2,)),
        ],
        compiler_params=pltpu.CompilerParams(
            collective_id=1, has_side_effects=True, vmem_limit_bytes=vmem_bytes - own.size * 4 - (1 << 20)
        ),
    )(own, spill, dropped, both)


def solve_kernel(
    live_ref,
    shift_ref,
    own_hbm,
    right_hbm,
    below_hbm,
    corner_hbm,
    probe_hbm,
    measured_hbm,
    rows_hbm,
    cols_hbm,
    out_hbm,
    out_right_hbm,
    out_below_hbm,
    out_corner_hbm,
    field,
    grown,
    mixed,
    spectra,
    backs,
    right_ref,
    below_ref,
    corner_ref,
    probe_ref,
    measured_ref,
    rows_ref,
    cols_ref,
    fetches,
    puts,
):
    tile_len = own_hbm.shape[1]
    side_len = probe_ref.shape[1]
    part = side_len // RADIX
    own_blocks = tile_len // LANES
    side_blocks = side_len // LANES
    lane = lax.broadcasted_iota(jnp.int32, (1, LANES), 1)

    loads = [
        pltpu.make_async_copy(source, target, fetches.at[i])
        for i, (source, target) in enumerate(
            (
                (below_hbm, below_ref),
                (right_hbm, right_ref),
                (corner_hbm, corner_ref),
                (probe_hbm, probe_ref),
                (rows_hbm, rows_ref),
                (cols_hbm, cols_ref),
                (measured_hbm, measured_ref),
            )
        )
    ]
    for load in loads[:3]:
        load.start()
    pieces = [
        pltpu.make_async_copy(
            own_hbm.at[c, :, b * LANES : (b + 1) * LANES],
            field.at[c, b, :tile_len, :],
            fetches.at[len(loads) + c * own_blocks + b],
        )
        for c in range(2)
        for b in range(own_blocks)
    ]
    for load in pieces + loads[3:]:
        load.start()
    grown[...] = jnp.zeros_like(grown)
    loads[0].wait()
    for c in range(2):
        for b in range(own_blocks):
            at = slice(b * LANES, (b + 1) * LANES)
            field[c, b, tile_len:, :] = below_ref[c, :, at].astype(jnp.float32)
    loads[1].wait()
    loads[2].wait()
    for c in range(2):
        for b in range(side_blocks):
            at = slice(b * LANES, (b + 1) * LANES)
            field[c, own_blocks + b, :tile_len, :] = right_ref[c, :, at].astype(jnp.float32)
            field[c, own_blocks + b, tile_len:, :] = corner_ref[c, :, at].astype(jnp.float32)
    for load in pieces + loads[3:]:
        load.wait()

    def one_slot(slot, carry):
        row = shift_ref[0, slot]
        col = shift_ref[1, slot]
        block = lax.div(col, LANES)
        turn = lax.rem(col, LANES)
        back_turn = lax.rem(LANES - turn, LANES)
        keep = lane < LANES - turn
        enter = lane >= turn
        height = 16

        def load_rows(i, carry):
            at = pl.multiple_of(i * height, height)
            waves = []
            for p in range(RADIX):
                cuts = []
                for c in range(2):
                    turned = [
                        pltpu.roll(
                            field[c, block + b, pl.ds(row + at + p * part, height), :], back_turn, 1
                        )
                        for b in range(side_blocks + 1)
                    ]
                    cuts.append(
                        [jnp.where(keep, turned[b], turned[b + 1]) for b in range(side_blocks)]
                    )
                blocks = []
                for b in range(side_blocks):
                    cols = slice(b * LANES, (b + 1) * LANES)
                    probe_re = probe_ref[0, pl.ds(at + p * part, height), cols]
                    probe_im = probe_ref[1, pl.ds(at + p * part, height), cols]
                    re, im = cuts[0][b], cuts[1][b]
                    blocks.append((probe_re * re - probe_im * im, probe_re * im + probe_im * re))
                waves.append(blocks)
            for b in range(side_blocks):
                cols = slice(b * LANES, (b + 1) * LANES)
                sums = butterfly([waves[p][b] for p in range(RADIX)], -1)
                for q in range(RADIX):
                    mixed[q, pl.ds(at, height), cols] = sums[q][0].astype(jnp.bfloat16)
                    mixed[q, pl.ds(at + part, height), cols] = sums[q][1].astype(jnp.bfloat16)
            return carry

        lax.fori_loop(0, part // height, load_rows, 0, unroll=part // height)

        for q in range(RADIX):
            half = dot(rows_ref[q], mixed[q])
            parts = [
                (half[:part, p * part : (p + 1) * part], half[part:, p * part : (p + 1) * part])
                for p in range(RADIX)
            ]
            misfits = []
            for other, (re, im) in enumerate(butterfly(parts, -1)):
                far = dot(jnp.concatenate([re, im], axis=1).astype(jnp.bfloat16), cols_ref[other])
                far_re, far_im = far[:, :part], far[:, part:]
                seen = measured_ref[
                    slot, q * part : (q + 1) * part, other * part : (other + 1) * part
                ].astype(jnp.float32)
                misfit = far_re * far_re + far_im * far_im - seen
                misfits.append(
                    jnp.concatenate([misfit * far_re, misfit * far_im], axis=0).astype(jnp.bfloat16)
                )
            spectra[q] = dot(cols_ref[q], jnp.concatenate(misfits, axis=1))

        def mix_rows(i, carry):
            at = pl.multiple_of(i * height, height)
            for other in range(RADIX):
                cols = slice(other * part, (other + 1) * part)
                parts = [
                    (spectra[q, pl.ds(at, height), cols], spectra[q, pl.ds(at + part, height), cols])
                    for q in range(RADIX)
                ]
                for p, (re, im) in enumerate(butterfly(parts, 1)):
                    backs[other, pl.ds(at + p * part, height), :] = jnp.concatenate(
                        [re, im], axis=1
                    ).astype(jnp.bfloat16)
            return carry

        lax.fori_loop(0, part // height, mix_rows, 0, unroll=part // height)

        def add_rows(i, carry):
            tall = 256
            at = pl.multiple_of(i * tall, tall)
            parts = []
            for other in range(RADIX):
                grad = dot(backs[other, pl.ds(at, tall), :], rows_ref[other])
                parts.append((grad[:, :part], grad[:, part:]))
            turned = [[], []]
            for b, (re, im) in enumerate(butterfly(parts, 1)):
                cols = slice(b * part, (b + 1) * part)
                probe_re = probe_ref[0, pl.ds(at, tall), cols]
                probe_im = probe_ref[1, pl.ds(at, tall), cols]
                turned[0].append(pltpu.roll(probe_re * re + probe_im * im, turn, 1))
                turned[1].append(pltpu.roll(probe_re * im - probe_im * re, turn, 1))
            for c in range(2):
                for b in range(side_blocks + 1):
                    if b == 0:
                        value = jnp.where(enter, turned[c][0], 0.0)
                    elif b == side_blocks:
                        value = jnp.where(enter, 0.0, turned[c][b - 1])
                    else:
                        value = jnp.where(enter, turned[c][b], turned[c][b - 1])
                    grown[c, block + b, pl.ds(row + at, tall), :] += value
            return carry

        lax.fori_loop(0, side_len // 256, add_rows, 0)
        return carry

    lax.fori_loop(0, live_ref[0, lax.axis_index("scan")], one_slot, 0)

    stores = [
        pltpu.make_async_copy(
            grown.at[c, b, :tile_len, :],
            out_hbm.at[c, :, b * LANES : (b + 1) * LANES],
            puts.at[3 + c * own_blocks + b],
        )
        for c in range(2)
        for b in range(own_blocks)
    ]
    for store in stores:
        store.start()
    for c in range(2):
        for b in range(side_blocks):
            at = slice(b * LANES, (b + 1) * LANES)
            corner_ref[c, :, at] = grown[c, own_blocks + b, tile_len:, :].astype(jnp.bfloat16)
            right_ref[c, :, at] = grown[c, own_blocks + b, :tile_len, :].astype(jnp.bfloat16)
    stores.append(pltpu.make_async_copy(corner_ref, out_corner_hbm, puts.at[0]))
    stores.append(pltpu.make_async_copy(right_ref, out_right_hbm, puts.at[1]))
    stores[-2].start()
    stores[-1].start()
    for c in range(2):
        for b in range(own_blocks):
            at = slice(b * LANES, (b + 1) * LANES)
            below_ref[c, :, at] = grown[c, b, tile_len:, :].astype(jnp.bfloat16)
    stores.append(pltpu.make_async_copy(below_ref, out_below_hbm, puts.at[2]))
    stores[-1].start()
    for store in stores:
        store.wait()


def solve(live_counts, shifts, own, right, below, corner, probe, measured, tables):
    tile_len = own.shape[1]
    side_len = probe.shape[1]
    blocks = (tile_len + side_len) // LANES
    smem = pl.BlockSpec(memory_space=pltpu.SMEM)
    hbm = pl.BlockSpec(memory_space=pltpu.HBM)
    part = side_len // RADIX
    copies = 2 * (tile_len // LANES)
    return pl.pallas_call(
        solve_kernel,
        out_shape=[
            jax.ShapeDtypeStruct(own.shape, jnp.float32),
            jax.ShapeDtypeStruct(right.shape, jnp.bfloat16),
            jax.ShapeDtypeStruct(below.shape, jnp.bfloat16),
            jax.ShapeDtypeStruct(corner.shape, jnp.bfloat16),
        ],
        in_specs=[smem, smem] + [hbm] * 8,
        out_specs=[hbm] * 4,
        scratch_shapes=[
            pltpu.VMEM((2, blocks, tile_len + side_len, LANES), jnp.float32),
            pltpu.VMEM((2, blocks, tile_len + side_len, LANES), jnp.float32),
            pltpu.VMEM((RADIX, 2 * part, side_len), jnp.bfloat16),
            pltpu.VMEM((RADIX, 2 * part, side_len), jnp.float32),
            pltpu.VMEM((RADIX, side_len, 2 * part), jnp.bfloat16),
            pltpu.VMEM(right.shape, jnp.bfloat16),
            pltpu.VMEM(below.shape, jnp.bfloat16),
            pltpu.VMEM(corner.shape, jnp.bfloat16),
            pltpu.VMEM(probe.shape, jnp.float32),
            pltpu.VMEM(measured.shape, jnp.bfloat16),
            pltpu.VMEM(tables[0].shape, jnp.bfloat16),
            pltpu.VMEM(tables[1].shape, jnp.bfloat16),
            pltpu.SemaphoreType.DMA((7 + copies,)),
            pltpu.SemaphoreType.DMA((3 + copies,)),
        ],
        compiler_params=pltpu.CompilerParams(vmem_limit_bytes=vmem_bytes),
    )(live_counts, shifts, own, right, below, corner, probe, measured, *tables)


def shards(axes, object_slab, probe_field, intensities, offsets, live_count):
    right, below, corner, measured = gather(axes, object_slab, intensities[0, 0])
    tables = residue_tables(probe_field.shape[-1])
    own, spill, dropped, both = solve(
        live_count.T, offsets[0, 0].T, object_slab, right, below, corner, probe_field, measured, tables
    )
    return scatter(axes, own, spill, dropped, both)


def solution(mesh):
    placed = (
        P(None, "tile", "scan"),
        P(),
        P("scan", "tile", None, None, None),
        P("scan", "tile", None, None),
        P(None, "tile"),
    )
    axes = tuple((name, mesh.shape[name]) for name in ("scan", "tile"))
    return jax.shard_map(
        functools.partial(shards, axes), mesh=mesh, in_specs=placed, out_specs=P(None, "tile", "scan"), check_vma=False
    )
```

profile of v0, /device:TPU:16, one launch (start us, length us, event | category | flops | bytes accessed | tf_op | source)
XLA Modules:
  0.0 119.5 jit_solution(11854167041442394072)
XLA Ops:
  0.0 40.7 %shard_map.91 = (bf16[2,768,512]{2,1,0:T(8,128)(2,1)}, bf16[2,512,768]{2,1,0:T(8,128)(2,1)}, bf16[2,512,512]{2,1,0:T(8,128)(2,1)}, bf16[6,512,512]{2,1,0:T(8,128)(2,1)}) custom-call(f32[2,768,768]{2,1,0:T(8,128)} %own_hbm.3, bf16[6,512,512]{2,1,0:T(8,128)(2,1)} %bitcast.5, bf16[512,512]{1,0:T(8,128)(2,1)} %constant.8.clone.sort_hbm, ...), custom_call_target="tpu_custom_call" | custom-call | tf_op jit(solution)/shard_map/pallas_call | solution.py:245
  40.7 36.8 %shard_map.92 = (f32[2,768,768]{2,1,0:T(8,128)}, bf16[2,768,512]{2,1,0:T(8,128)(2,1)}, bf16[2,512,768]{2,1,0:T(8,128)(2,1)}, bf16[2,512,512]{2,1,0:T(8,128)(2,1)}) custom-call(s32[1,8]{1,0:T(1,128)} %bitcast.7, s32[2,6]{1,0:T(2,128)} %bitcast.6, f32[2,768,768]{2,1,0:T(8,128)} %own_hbm.3, bf16[2,768,512]{2,1,0:T(8,128)(2,1)} %get-tuple-element.13.right_hbm, ...), custom_call_target="tpu_custom_call" | custom-call | tf_op jit(solution)/shard_map/pallas_call | solution.py:613
  77.6 39.7 %shard_map.93 = f32[2,768,768]{2,1,0:T(8,128)S(1)} custom-call(f32[2,768,768]{2,1,0:T(8,128)} %get-tuple-element.17.own_hbm, bf16[2,768,512]{2,1,0:T(8,128)(2,1)} %get-tuple-element.18.spill_hbm, bf16[2,512,768]{2,1,0:T(8,128)(2,1)} %get-tuple-element.19.drop_hbm, bf16[2,512,512]{2,1,0:T(8,128)(2,1)} %get-tuple-element.20.both_hbm), custom_call_target="tpu_custom_call" | custom-call | tf_op jit(solution)/shard_map/pallas_call | solution.py:366
  117.3 2.2 %copy.11 = f32[2,768,768]{2,1,0:T(8,128)} copy(f32[2,768,768]{2,1,0:T(8,128)S(1)} %shard_map.93) | data formatting | bytes 9437184
where the time goes:
time: 120 us; the launch traced here: 119 us
  Pallas kernels  117 us (98%)
  local copies, waits for them, and re-layouts  2.19 us (2%)
    pallas_call x1, Pallas kernels, gather(): pl.pallas_call(functools.partial(gather_kernel, axes), out_shape=[jax.Sha...  40.7 us
    pallas_call x1, Pallas kernels, scatter(): pl.pallas_call(functools.partial(scatter_kernel, axes), out_shape=pltpu.V...  39.7 us
    pallas_call x1, Pallas kernels, solve(): pl.pallas_call(solve_kernel, out_shape=[jax.ShapeDtypeStruct(own.shape, j...  36.8 us

commit v1 on v0

v1 whole, which is shorter than its diff:
```python
import functools
import math

import jax
import jax.numpy as jnp
import numpy as np
from jax import lax
from jax.experimental import pallas as pl
from jax.experimental.pallas import tpu as pltpu
from jax.sharding import PartitionSpec as P

RADIX = 4
LANES = 128
GROUP = 16
TALL = 256


def residue_tables(side_len):
    part = side_len // RADIX
    freq = np.arange(side_len).reshape(part, RADIX).T
    across = np.arange(part)
    phase = (freq[:, :, None] * across[None, None, :] % side_len) * (2.0 * math.pi / side_len)
    factor = 1.0 / math.sqrt(side_len)
    cos = np.cos(phase) * factor
    sin = np.sin(phase) * factor
    rows = np.concatenate(
        [np.concatenate([cos, sin], axis=2), np.concatenate([-sin, cos], axis=2)], axis=1
    ).astype(np.float32)
    return jnp.asarray(rows, jnp.bfloat16), jnp.asarray(rows.swapaxes(1, 2), jnp.bfloat16)


def sorted_by_residue(side_len):
    at = np.arange(side_len)
    source = at % (side_len // RADIX) * RADIX + at // (side_len // RADIX)
    sort = (source[:, None] == at[None, :]).astype(np.float32)
    return jnp.asarray(sort, jnp.bfloat16), jnp.asarray(sort.T, jnp.bfloat16)


def dot(a, b):
    return jnp.dot(a, b, preferred_element_type=jnp.float32)


def butterfly(parts, sign):
    (r0, i0), (r1, i1), (r2, i2), (r3, i3) = parts
    ar, ai, br, bi = r0 + r2, i0 + i2, r1 + r3, i1 + i3
    cr, ci, dr, di = r0 - r2, i0 - i2, r1 - r3, i1 - i3
    plus = (cr - di, ci + dr)
    minus = (cr + di, ci - dr)
    first, third = (plus, minus) if sign > 0 else (minus, plus)
    return [(ar + br, ai + bi), first, (ar - br, ai - bi), third]


def neighbours(axes):
    result = []
    for name, count in axes:
        me = lax.axis_index(name)
        result.append((me > 0, {name: me - 1}, me < count - 1, {name: me + 1}))
    return result


def meet(peers):
    barrier = pltpu.get_barrier_semaphore()
    for has_low, low, has_high, high in peers:
        for there, peer in ((has_low, low), (has_high, high)):

            @pl.when(there)
            def _(peer=peer):
                pl.semaphore_signal(
                    barrier, inc=1, device_id=peer, device_id_type=pl.DeviceIdType.MESH
                )

    count = sum(
        there.astype(jnp.int32) for has_low, _, has_high, _ in peers for there in (has_low, has_high)
    )
    pl.semaphore_wait(barrier, count)


def remote(source, target, sends, receives, index, peer):
    return pltpu.make_async_remote_copy(
        src_ref=source,
        dst_ref=target,
        send_sem=sends.at[index],
        recv_sem=receives.at[index],
        device_id=peer,
        device_id_type=pl.DeviceIdType.MESH,
    )


def quarter_turns(cos, sin, q):
    return ((cos, sin), (sin, -cos), (-cos, -sin), (-sin, cos))[q]


def in_place(mask, cos, sin, q):
    wrapped = quarter_turns(cos, sin, q)
    return jnp.where(mask, cos, wrapped[0]), jnp.where(mask, sin, wrapped[1])


def gather_kernel(
    axes,
    shift_ref,
    own_hbm,
    measured_hbm,
    probe_hbm,
    rows_hbm,
    cols_hbm,
    sort_hbm,
    unsort_hbm,
    field,
    probes,
    tables,
    arranged,
    grown,
    own,
    measured,
    extended,
    rows_ref,
    cols_ref,
    doubled,
    sort,
    unsort,
    sends,
    receives,
    fetches,
):
    slots, side_len = measured.shape[:2]
    tile_len = own.shape[1]
    part = side_len // RADIX
    own_blocks = tile_len // LANES
    side_blocks = side_len // LANES
    scan, tile = neighbours(axes)
    has_left, left, has_right, _ = scan
    has_up, up, has_down, _ = tile
    first = pltpu.make_async_copy(
        own_hbm.at[:, :side_len, :side_len], own.at[:, :side_len, :side_len], fetches.at[0]
    )
    second = pltpu.make_async_copy(
        own_hbm.at[:, side_len:, :side_len], own.at[:, side_len:, :side_len], fetches.at[1]
    )
    third = pltpu.make_async_copy(
        own_hbm.at[:, :side_len, side_len:], own.at[:, :side_len, side_len:], fetches.at[2]
    )
    fourth = pltpu.make_async_copy(
        own_hbm.at[:, side_len:, side_len:], own.at[:, side_len:, side_len:], fetches.at[3]
    )
    constants = [
        pltpu.make_async_copy(source, target, fetches.at[4 + i])
        for i, (source, target) in enumerate(
            (
                (sort_hbm, sort),
                (unsort_hbm, unsort),
                (measured_hbm, measured),
                (rows_hbm, rows_ref),
                (cols_hbm, cols_ref),
            )
        )
    ]
    for c in range(2):
        for b in range(side_blocks):
            cols = slice(b * LANES, (b + 1) * LANES)
            for source, target in (
                (probe_hbm.at[c, :, cols], extended.at[c, b, GROUP:, :]),
                (probe_hbm.at[c, side_len - GROUP :, cols], extended.at[c, b, :GROUP, :]),
            ):
                constants.append(
                    pltpu.make_async_copy(source, target, fetches.at[4 + len(constants)])
                )
    for load in [first, second, third, fourth] + constants:
        load.start()
    near = slice(0, side_blocks)
    far = slice(own_blocks, own_blocks + side_blocks)
    top = remote(
        field.at[:, near, :side_len, :], field.at[:, far, :side_len, :], sends, receives, 0, left
    )
    rest = remote(
        field.at[:, near, side_len:tile_len, :],
        field.at[:, far, side_len:tile_len, :],
        sends,
        receives,
        1,
        left,
    )
    under = remote(
        field.at[:, :own_blocks, :side_len, :],
        field.at[:, :own_blocks, tile_len:, :],
        sends,
        receives,
        2,
        up,
    )
    across = remote(
        field.at[:, far, :side_len, :], field.at[:, far, tile_len:, :], sends, receives, 3, up
    )

    def narrow(blocks, at):
        for c in range(2):
            for b in blocks:
                field[c, b, at, :] = own[c, at, b * LANES : (b + 1) * LANES].astype(jnp.bfloat16)

    first.wait()
    narrow(range(side_blocks), slice(0, side_len))
    meet((scan, tile))

    @pl.when(has_left)
    def _():
        top.start()

    second.wait()
    third.wait()
    narrow(range(side_blocks), slice(side_len, tile_len))
    narrow(range(side_blocks, own_blocks), slice(0, side_len))

    @pl.when(has_left)
    def _():
        rest.start()

    @pl.when(has_up)
    def _():
        under.start()

    @pl.when(jnp.logical_not(has_right))
    def _():
        field[:, far, :tile_len, :] = jnp.zeros(
            (2, side_blocks, tile_len, LANES), jnp.bfloat16
        )

    @pl.when(jnp.logical_not(has_down))
    def _():
        field[:, :, tile_len:, :] = jnp.zeros(
            (2, own_blocks + side_blocks, side_len, LANES), jnp.bfloat16
        )

    fourth.wait()
    narrow(range(side_blocks, own_blocks), slice(side_len, tile_len))
    for load in constants:
        load.wait()

    def sort_slot(slot, carry):
        rows = dot(sort[...], measured[slot]).astype(jnp.bfloat16)
        both = dot(rows, unsort[...]).astype(jnp.bfloat16)
        for b in range(RADIX):
            arranged[slot, b] = both[:, b * part : (b + 1) * part]
        return carry

    lax.fori_loop(0, slots, sort_slot, 0)

    grown[...] = jnp.zeros_like(grown)
    for q in range(RADIX):
        for i in range(2):
            for at in (0, part):
                doubled[q, i, at : at + part, :] = cols_ref[
                    q, i * part : (i + 1) * part, :part
                ].astype(jnp.float32)

    lane = lax.broadcasted_iota(jnp.int32, (1, LANES), 1)
    line = lax.broadcasted_iota(jnp.int32, (part, LANES), 0)
    chunk = 32

    def prepare(slot, carry):
        lift = lax.rem(shift_ref[0, slot], GROUP)
        turn = lax.rem(shift_ref[1, slot], LANES)

        def move_probe(i, carry):
            at = pl.multiple_of(i * chunk, chunk)
            for c in range(2):
                turned = [
                    pltpu.roll(extended[c, b, pl.ds(GROUP - lift + at, chunk), :], turn, 1)
                    for b in range(side_blocks)
                ]
                for b in range(side_blocks):
                    probes[slot, c, b, pl.ds(at, chunk), :] = jnp.where(
                        lane >= turn, turned[b], turned[b - 1]
                    )
            return carry

        lax.fori_loop(0, side_len // chunk, move_probe, 0)
        for k, by in enumerate((lift, turn)):
            for q in range(RADIX):
                cos = pltpu.roll(rows_ref[q, :part, :part].astype(jnp.float32), by, 1)
                sin = pltpu.roll(rows_ref[q, :part, part:].astype(jnp.float32), by, 1)
                cos, sin = in_place(lane >= by, cos, sin, q)
                tables[slot, 0, k, q, 0, :part, :] = cos.astype(jnp.bfloat16)
                tables[slot, 0, k, q, 1, :part, :] = sin.astype(jnp.bfloat16)
                tables[slot, 0, k, q, 0, part:, :] = (-sin).astype(jnp.bfloat16)
                tables[slot, 0, k, q, 1, part:, :] = cos.astype(jnp.bfloat16)
                cos = doubled[q, 0, pl.ds(part - by, part), :]
                sin = doubled[q, 1, pl.ds(part - by, part), :]
                cos, sin = in_place(line >= by, cos, sin, q)
                tables[slot, 1, k, q, 0, :part, :] = cos.astype(jnp.bfloat16)
                tables[slot, 1, k, q, 1, :part, :] = (-sin).astype(jnp.bfloat16)
                tables[slot, 1, k, q, 0, part:, :] = sin.astype(jnp.bfloat16)
                tables[slot, 1, k, q, 1, part:, :] = cos.astype(jnp.bfloat16)
        return carry

    lax.fori_loop(0, slots, prepare, 0)

    @pl.when(has_right)
    def _():
        top.wait_recv()

    @pl.when(has_up)
    def _():
        across.start()

    @pl.when(has_down)
    def _():
        under.wait_recv()

    @pl.when(has_right)
    def _():
        rest.wait_recv()

    @pl.when(has_down)
    def _():
        across.wait_recv()

    @pl.when(has_left)
    def _():
        top.wait_send()
        rest.wait_send()

    @pl.when(has_up)
    def _():
        under.wait_send()
        across.wait_send()


def gather(axes, shifts, own, measured, probe, tables):
    slots, side_len = measured.shape[:2]
    tile_len = own.shape[1]
    span = tile_len + side_len
    part = side_len // RADIX
    side_blocks = side_len // LANES
    hbm = pl.BlockSpec(memory_space=pltpu.HBM)
    vmem = pl.BlockSpec(memory_space=pltpu.VMEM)
    table = (slots, 2, 2, RADIX, 2, 2 * part, part)
    scratch = [
        (own.shape, jnp.float32),
        (measured.shape, jnp.bfloat16),
        ((2, side_blocks, side_len + GROUP, LANES), jnp.float32),
        (tables[0].shape, jnp.bfloat16),
        (tables[1].shape, jnp.bfloat16),
        ((RADIX, 2, 2 * part, part), jnp.float32),
        ((side_len, side_len), jnp.bfloat16),
        ((side_len, side_len), jnp.bfloat16),
    ]
    call = pl.pallas_call(
        functools.partial(gather_kernel, axes),
        out_shape=[
            pltpu.VMEM((2, span // LANES, span, LANES), jnp.bfloat16),
            pltpu.VMEM((slots, 2, side_blocks, side_len, LANES), jnp.float32),
            pltpu.VMEM(table, jnp.bfloat16),
            pltpu.VMEM((slots, RADIX, side_len, part), jnp.bfloat16),
            pltpu.VMEM((2, span // LANES, span, LANES), jnp.float32),
        ],
        in_specs=[pl.BlockSpec(memory_space=pltpu.SMEM)] + [hbm] * 7,
        out_specs=[vmem] * 5,
        scratch_shapes=[pltpu.VMEM(*each) for each in scratch]
        + [
            pltpu.SemaphoreType.DMA((4,)),
            pltpu.SemaphoreType.DMA((4,)),
            pltpu.SemaphoreType.DMA((9 + 4 * side_blocks,)),
        ],
        compiler_params=pltpu.CompilerParams(
            collective_id=0, has_side_effects=True, vmem_limit_bytes=room(scratch)
        ),
    )
    prepared = call(shifts, own, measured, probe, *tables, *sorted_by_residue(side_len))
    held = [pltpu.with_memory_space_constraint(each, pltpu.VMEM) for each in prepared]
    return held, room(scratch)


def room(scratch):
    return sum(math.prod(shape) * jnp.dtype(kind).itemsize for shape, kind in scratch) + (1 << 20)


def scatter_kernel(
    axes,
    grown,
    total,
    spill,
    dropped,
    both,
    landed,
    from_left,
    from_up,
    sends,
    receives,
):
    side_len = landed.shape[2]
    tile_len = total.shape[1]
    own_blocks = tile_len // LANES
    side_blocks = side_len // LANES
    scan, tile = neighbours(axes)
    has_left, _, has_right, right = scan
    has_up, _, has_down, down = tile
    corner = remote(both, landed, sends, receives, 0, down)
    under = remote(dropped, from_up, sends, receives, 1, down)
    rest = remote(
        spill.at[:, :, side_len:, :], from_left.at[:, :, side_len:, :], sends, receives, 2, right
    )
    top = remote(
        spill.at[:, :, :side_len, :], from_left.at[:, :, :side_len, :], sends, receives, 3, right
    )
    both[...] = grown[:, own_blocks:, tile_len:, :].astype(jnp.bfloat16)
    meet((scan, tile))

    @pl.when(has_down)
    def _():
        corner.start()

    spill[:, :, side_len:, :] = grown[:, own_blocks:, side_len:tile_len, :].astype(jnp.bfloat16)

    @pl.when(has_right)
    def _():
        rest.start()

    dropped[...] = grown[:, :own_blocks, tile_len:, :].astype(jnp.bfloat16)

    @pl.when(has_down)
    def _():
        under.start()

    @pl.when(jnp.logical_not(has_up))
    def _():
        landed[...] = jnp.zeros_like(landed)

    for c in range(2):
        for b in range(own_blocks):
            total[c, :, b * LANES : (b + 1) * LANES] = grown[c, b, :tile_len, :]

    @pl.when(has_up)
    def _():
        corner.wait_recv()

    spill[:, :, :side_len, :] = (
        grown[:, own_blocks:, :side_len, :] + landed[...].astype(jnp.float32)
    ).astype(jnp.bfloat16)

    @pl.when(has_right)
    def _():
        top.start()

    def add(blocks, at, source):
        for c in range(2):
            for b in blocks:
                total[c, at, b * LANES : (b + 1) * LANES] += source[c, b, at, :].astype(jnp.float32)

    @pl.when(has_left)
    def _():
        rest.wait_recv()
        add(range(side_blocks), slice(side_len, tile_len), from_left)

    @pl.when(has_up)
    def _():
        under.wait_recv()
        add(range(own_blocks), slice(0, side_len), from_up)

    @pl.when(has_left)
    def _():
        top.wait_recv()
        add(range(side_blocks), slice(0, side_len), from_left)

    @pl.when(has_right)
    def _():
        rest.wait_send()
        top.wait_send()

    @pl.when(has_down)
    def _():
        corner.wait_send()
        under.wait_send()


def scatter(axes, grown, tile_len):
    span = grown.shape[2]
    side_len = span - tile_len
    own_blocks = tile_len // LANES
    side_blocks = side_len // LANES
    vmem = pl.BlockSpec(memory_space=pltpu.VMEM)
    scratch = [
        ((2, side_blocks, tile_len, LANES), jnp.bfloat16),
        ((2, own_blocks, side_len, LANES), jnp.bfloat16),
        ((2, side_blocks, side_len, LANES), jnp.bfloat16),
        ((2, side_blocks, side_len, LANES), jnp.bfloat16),
        ((2, side_blocks, tile_len, LANES), jnp.bfloat16),
        ((2, own_blocks, side_len, LANES), jnp.bfloat16),
    ]
    return pl.pallas_call(
        functools.partial(scatter_kernel, axes),
        out_shape=pltpu.VMEM((2, tile_len, tile_len), jnp.float32),
        in_specs=[vmem],
        out_specs=vmem,
        scratch_shapes=[pltpu.VMEM(*each) for each in scratch]
        + [pltpu.SemaphoreType.DMA((4,)), pltpu.SemaphoreType.DMA((4,))],
        compiler_params=pltpu.CompilerParams(
            collective_id=1, has_side_effects=True, vmem_limit_bytes=room(scratch)
        ),
    )(grown)


def side_by_side(*blocks):
    return jnp.concatenate(blocks, axis=1)


def solve_kernel(
    live_ref,
    shift_ref,
    field,
    probes,
    tables,
    measured,
    zeros,
    grown,
    mixed,
    halves,
    misfits,
    spectra,
    backs,
):
    side_len = probes.shape[3]
    part = side_len // RADIX
    side_blocks = side_len // LANES
    lane = lax.broadcasted_iota(jnp.int32, (1, LANES), 1)
    line = lax.broadcasted_iota(jnp.int32, (GROUP, LANES), 0)

    def one_slot(slot, carry):
        row = shift_ref[0, slot]
        col = shift_ref[1, slot]
        lift = lax.rem(row, GROUP)
        turn = lax.rem(col, LANES)
        base = pl.multiple_of(row - lift, GROUP)
        block = lax.div(col, LANES)
        stay = lane >= turn
        below = line >= lift

        def table(side, kind, q):
            return side_by_side(tables[slot, side, kind, q, 0], tables[slot, side, kind, q, 1])

        def piece(c, b, at):
            def cut(b):
                start = pl.multiple_of(base + at, GROUP)
                value = field[c, block + b, pl.ds(start, GROUP), :].astype(jnp.float32)
                if at == 0:
                    start = pl.multiple_of(base + side_len, GROUP)
                    wrapped = field[c, block + b, pl.ds(start, GROUP), :].astype(jnp.float32)
                    value = jnp.where(below, value, wrapped)
                return value

            return cut(b) if b else jnp.where(stay, cut(0), cut(side_blocks))

        for at in range(0, part, GROUP):
            for b in range(side_blocks):
                waves = []
                for p in range(RADIX):
                    here = at + p * part
                    re, im = piece(0, b, here), piece(1, b, here)
                    probe_re = probes[slot, 0, b, here : here + GROUP, :]
                    probe_im = probes[slot, 1, b, here : here + GROUP, :]
                    waves.append((probe_re * re - probe_im * im, probe_re * im + probe_im * re))
                for q, (re, im) in enumerate(butterfly(waves, -1)):
                    mixed[q, b, at : at + GROUP, :] = re.astype(jnp.bfloat16)
                    mixed[q, b, at + part : at + part + GROUP, :] = im.astype(jnp.bfloat16)

        for q in range(RADIX):
            half = dot(table(0, 0, q), side_by_side(*(mixed[q, b] for b in range(RADIX))))
            parts = [
                (half[:part, p * part : (p + 1) * part], half[part:, p * part : (p + 1) * part])
                for p in range(RADIX)
            ]
            for other, (re, im) in enumerate(butterfly(parts, -1)):
                halves[other, 0, q * part : (q + 1) * part, :] = re.astype(jnp.bfloat16)
                halves[other, 1, q * part : (q + 1) * part, :] = im.astype(jnp.bfloat16)

        for other in range(RADIX):
            far = dot(side_by_side(halves[other, 0], halves[other, 1]), table(1, 1, other))
            for q in range(RADIX):
                rows = slice(q * part, (q + 1) * part)
                far_re, far_im = far[rows, :part], far[rows, part:]
                seen = measured[slot, other, rows, :].astype(jnp.float32)
                misfit = far_re * far_re + far_im * far_im - seen
                misfits[q, other, :part, :] = (misfit * far_re).astype(jnp.bfloat16)
                misfits[q, other, part:, :] = (misfit * far_im).astype(jnp.bfloat16)

        for q in range(RADIX):
            mixture = dot(
                table(1, 0, q), side_by_side(*(misfits[q, b] for b in range(RADIX)))
            )
            for b in range(RADIX):
                spectra[q, b] = mixture[:, b * part : (b + 1) * part]

        for at in range(0, part, GROUP):
            for other in range(RADIX):
                parts = [
                    (spectra[q, other, at : at + GROUP, :], spectra[q, other, part + at : part + at + GROUP, :])
                    for q in range(RADIX)
                ]
                for p, (re, im) in enumerate(butterfly(parts, 1)):
                    here = slice(at + p * part, at + p * part + GROUP)
                    backs[other, 0, here, :] = re.astype(jnp.bfloat16)
                    backs[other, 1, here, :] = im.astype(jnp.bfloat16)

        tall = TALL

        def add(c, b, at, value):
            where = pl.ds(pl.multiple_of(base + at, GROUP), value.shape[0])
            grown[c, block + b, where, :] += value

        def add_wrapped(c, b, at, value):
            if at == 0:
                add(c, b, 0, jnp.where(below, value[:GROUP], 0.0))
                add(c, b, side_len, jnp.where(below, 0.0, value[:GROUP]))
                add(c, b, GROUP, value[GROUP:])
            else:
                add(c, b, at, value)

        for at in range(0, side_len, tall):
            parts = []
            for other in range(RADIX):
                back = side_by_side(
                    backs[other, 0, at : at + tall, :], backs[other, 1, at : at + tall, :]
                )
                grad = dot(back, table(0, 1, other))
                parts.append((grad[:, :part], grad[:, part:]))
            for b, (re, im) in enumerate(butterfly(parts, 1)):
                probe_re = probes[slot, 0, b, at : at + tall, :]
                probe_im = probes[slot, 1, b, at : at + tall, :]
                values = (probe_re * re + probe_im * im, probe_re * im - probe_im * re)
                for c, value in enumerate(values):
                    if b == 0:
                        add_wrapped(c, 0, at, jnp.where(stay, value, 0.0))
                        add_wrapped(c, side_blocks, at, jnp.where(stay, 0.0, value))
                    else:
                        add_wrapped(c, b, at, value)
        return carry

    lax.fori_loop(0, live_ref[0, lax.axis_index("scan")], one_slot, 0)


def solve(live_counts, shifts, prepared, limit):
    grown = prepared[-1]
    side_len = prepared[1].shape[3]
    part = side_len // RADIX
    smem = pl.BlockSpec(memory_space=pltpu.SMEM)
    vmem = pl.BlockSpec(memory_space=pltpu.VMEM)
    wide = (RADIX, RADIX, 2 * part, part)
    tall = (RADIX, 2, side_len, part)
    scratch = [
        (wide, jnp.bfloat16),
        (tall, jnp.bfloat16),
        (wide, jnp.bfloat16),
        (wide, jnp.float32),
        (tall, jnp.bfloat16),
    ]
    return pl.pallas_call(
        solve_kernel,
        out_shape=pltpu.VMEM(grown.shape, grown.dtype),
        in_specs=[smem, smem] + [vmem] * len(prepared),
        out_specs=vmem,
        scratch_shapes=[pltpu.VMEM(*each) for each in scratch],
        input_output_aliases={1 + len(prepared): 0},
        compiler_params=pltpu.CompilerParams(vmem_limit_bytes=limit),
    )(live_counts, shifts, *prepared)


def shards(axes, object_slab, probe_field, intensities, offsets, live_count):
    tables = residue_tables(probe_field.shape[-1])
    shifts = offsets[0, 0].T
    prepared, limit = gather(axes, shifts, object_slab, intensities[0, 0], probe_field, tables)
    grown = solve(live_count.T, shifts, prepared, limit)
    return scatter(axes, grown, object_slab.shape[1])


def solution(mesh):
    placed = (
        P(None, "tile", "scan"),
        P(),
        P("scan", "tile", None, None, None),
        P("scan", "tile", None, None),
        P(None, "tile"),
    )
    axes = tuple((name, mesh.shape[name]) for name in ("scan", "tile"))
    return jax.shard_map(
        functools.partial(shards, axes), mesh=mesh, in_specs=placed, out_specs=P(None, "tile", "scan"), check_vma=False
    )
```

time: 120 us -> 98.5 us (0.82)
  the two profiles are of different devices: /device:TPU:16 before, /device:TPU:8 now
where the time goes in v1:
time: 98.5 us; the launch traced here: 98.3 us
  Pallas kernels  96.1 us (98%)
  local copies, waits for them, and re-layouts  2.19 us (2%)
    pallas_call x1, Pallas kernels, scatter(): pl.pallas_call(functools.partial(scatter_kernel, axes), out_shape=pltpu.V...  52.5 us
    pallas_call x1, Pallas kernels, gather(): call(shifts, own, measured, probe, *tables, *sorted_by_residue(side_len))  40.4 us
    pallas_call x1, Pallas kernels, solve(): pl.pallas_call(solve_kernel, out_shape=pltpu.VMEM(grown.shape, grown.dtyp...  3.2 us
    unnamed x1, local copies, waits for them, and re-layouts  2.19 us

profile of v1, /device:TPU:8, one launch (start us, length us, event | category | flops | bytes accessed | tf_op | source)
XLA Modules:
  0.0 98.3 jit_solution(4592016644679953597)
XLA Ops:
  0.0 40.4 %shard_map.91 = (bf16[2,10,1280,128]{3,2,1,0:T(8,128)(2,1)S(1)}, f32[6,2,4,512,128]{4,3,2,1,0:T(8,128)S(1)}, bf16[6,2,2,4,2,256,128]{6,5,4,3,2,1,0:T(8,128)(2,1)...) custom-call(s32[2,6]{1,0:T(2,128)} %bitcast.6, f32[2,768,768]{2,1,0:T(8,128)} %own_hbm.1, ...), custom_call_target="tpu_custom_call" | custom-call | tf_op jit(solution)/shard_map/pallas_call | solution.py:367
  40.4 3.2 %shard_map.92.grown = f32[2,10,1280,128]{3,2,1,0:T(8,128)S(1)} custom-call(s32[1,8]{1,0:T(1,128)} %bitcast.8, s32[2,6]{1,0:T(2,128)} %bitcast.7, bf16[2,10,1280,128]{3,2,1,0:T(8,128)(2,1)S(1)} %get-tuple-element.10.field, f32[6,2,4,512,128]{4,3,2,1,0:T(8,128)S(1)} %get-tuple-element.11.probes, ...), custom_call_target="tpu_custom_call", output_to_operand_aliasing={{}: (6, {})} | custom-call | tf_op jit(solution)/shard_map/pallas_call | solution.py:654
  43.6 52.5 %shard_map.93 = f32[2,768,768]{2,1,0:T(8,128)S(1)} custom-call(f32[2,10,1280,128]{3,2,1,0:T(8,128)S(1)} %shard_map.92.grown), custom_call_target="tpu_custom_call" | custom-call | tf_op jit(solution)/shard_map/pallas_call | solution.py:488
  96.1 2.2 %copy.13 = f32[2,768,768]{2,1,0:T(8,128)} copy(f32[2,768,768]{2,1,0:T(8,128)S(1)} %shard_map.93) | data formatting | bytes 9437184

commit v2 on v1

--- a/solution.py
+++ b/solution.py
@@ -58,7 +58,7 @@
     return result
 
 
-def meet(peers):
+def greet(peers):
     barrier = pltpu.get_barrier_semaphore()
     for has_low, low, has_high, high in peers:
         for there, peer in ((has_low, low), (has_high, high)):
@@ -69,10 +69,12 @@
                     barrier, inc=1, device_id=peer, device_id_type=pl.DeviceIdType.MESH
                 )
 
+
+def all_here(peers):
     count = sum(
         there.astype(jnp.int32) for has_low, _, has_high, _ in peers for there in (has_low, has_high)
     )
-    pl.semaphore_wait(barrier, count)
+    pl.semaphore_wait(pltpu.get_barrier_semaphore(), count)
 
 
 def remote(source, target, sends, receives, index, peer):
@@ -130,6 +132,7 @@
     scan, tile = neighbours(axes)
     has_left, left, has_right, _ = scan
     has_up, up, has_down, _ = tile
+    greet((scan, tile))
     first = pltpu.make_async_copy(
         own_hbm.at[:, :side_len, :side_len], own.at[:, :side_len, :side_len], fetches.at[0]
     )
@@ -168,9 +171,26 @@
         load.start()
     near = slice(0, side_blocks)
     far = slice(own_blocks, own_blocks + side_blocks)
-    top = remote(
-        field.at[:, near, :side_len, :], field.at[:, far, :side_len, :], sends, receives, 0, left
-    )
+    halves = [
+        (c, slice(at, at + side_blocks // 2))
+        for c in range(2)
+        for at in range(0, side_blocks, side_blocks // 2)
+    ]
+
+    def moved(blocks):
+        return slice(blocks.start + own_blocks, blocks.stop + own_blocks)
+
+    tops = [
+        remote(
+            field.at[c, blocks, :side_len, :],
+            field.at[c, moved(blocks), :side_len, :],
+            sends,
+            receives,
+            3 + i,
+            left,
+        )
+        for i, (c, blocks) in enumerate(halves)
+    ]
     rest = remote(
         field.at[:, near, side_len:tile_len, :],
         field.at[:, far, side_len:tile_len, :],
@@ -187,9 +207,17 @@
         2,
         up,
     )
-    across = remote(
-        field.at[:, far, :side_len, :], field.at[:, far, tile_len:, :], sends, receives, 3, up
-    )
+    acrosses = [
+        remote(
+            field.at[c, moved(blocks), :side_len, :],
+            field.at[c, moved(blocks), tile_len:, :],
+            sends,
+            receives,
+            3 + len(halves) + i,
+            up,
+        )
+        for i, (c, blocks) in enumerate(halves)
+    ]
 
     def narrow(blocks, at):
         for c in range(2):
@@ -198,11 +226,12 @@
 
     first.wait()
     narrow(range(side_blocks), slice(0, side_len))
-    meet((scan, tile))
+    all_here((scan, tile))
 
     @pl.when(has_left)
     def _():
-        top.start()
+        for each in tops:
+            each.start()
 
     second.wait()
     third.wait()
@@ -293,35 +322,40 @@
 
     lax.fori_loop(0, slots, prepare, 0)
 
+    for top, across in zip(tops, acrosses):
+
+        @pl.when(has_right)
+        def _(top=top):
+            top.wait_recv()
+
+        @pl.when(has_up)
+        def _(across=across):
+            across.start()
+
+    @pl.when(has_down)
+    def _():
+        under.wait_recv()
+
     @pl.when(has_right)
     def _():
-        top.wait_recv()
+        rest.wait_recv()
+
+    @pl.when(has_down)
+    def _():
+        for each in acrosses:
+            each.wait_recv()
+
+    @pl.when(has_left)
+    def _():
+        for each in tops:
+            each.wait_send()
+        rest.wait_send()
 
     @pl.when(has_up)
     def _():
-        across.start()
-
-    @pl.when(has_down)
-    def _():
-        under.wait_recv()
-
-    @pl.when(has_right)
-    def _():
-        rest.wait_recv()
-
-    @pl.when(has_down)
-    def _():
-        across.wait_recv()
-
-    @pl.when(has_left)
-    def _():
-        top.wait_send()
-        rest.wait_send()
-
-    @pl.when(has_up)
-    def _():
         under.wait_send()
-        across.wait_send()
+        for each in acrosses:
+            each.wait_send()
 
 
 def gather(axes, shifts, own, measured, probe, tables):
@@ -356,8 +390,8 @@
         out_specs=[vmem] * 5,
         scratch_shapes=[pltpu.VMEM(*each) for each in scratch]
         + [
-            pltpu.SemaphoreType.DMA((4,)),
-            pltpu.SemaphoreType.DMA((4,)),
+            pltpu.SemaphoreType.DMA((3 + 8,)),
+            pltpu.SemaphoreType.DMA((3 + 8,)),
             pltpu.SemaphoreType.DMA((9 + 4 * side_blocks,)),
         ],
         compiler_params=pltpu.CompilerParams(
@@ -401,18 +435,18 @@
     top = remote(
         spill.at[:, :, :side_len, :], from_left.at[:, :, :side_len, :], sends, receives, 3, right
     )
+    greet((scan, tile))
+    spill[:, :, side_len:, :] = grown[:, own_blocks:, side_len:tile_len, :].astype(jnp.bfloat16)
     both[...] = grown[:, own_blocks:, tile_len:, :].astype(jnp.bfloat16)
-    meet((scan, tile))
+    all_here((scan, tile))
+
+    @pl.when(has_right)
+    def _():
+        rest.start()
 
     @pl.when(has_down)
     def _():
         corner.start()
-
-    spill[:, :, side_len:, :] = grown[:, own_blocks:, side_len:tile_len, :].astype(jnp.bfloat16)
-
-    @pl.when(has_right)
-    def _():
-        rest.start()
 
     dropped[...] = grown[:, :own_blocks, tile_len:, :].astype(jnp.bfloat16)
 

time: 98.5 us -> 94.5 us (0.959)
  Pallas kernels: 96.1 us -> 91.7 us
    pallas_call x1, Pallas kernels: 52.5 us -> 39.6 us  [scatter(): pl.pallas_call(functools.partial(scatter_kernel, axes), out_shape=pltpu.V...]
    pallas_call x1, Pallas kernels: 3.2 us -> 13.3 us  [solve(): pl.pallas_call(solve_kernel, out_shape=pltpu.VMEM(grown.shape, grown.dtyp...]
    pallas_call x1, Pallas kernels: 40.4 us -> 38.8 us  [gather(): call(shifts, own, measured, probe, *tables, *sorted_by_residue(side_len))]
where the time goes in v2:
time: 94.5 us; the launch traced here: 93.9 us
  Pallas kernels  91.7 us (97%)
  local copies, waits for them, and re-layouts  2.19 us (2%)
    pallas_call x1, Pallas kernels, scatter(): pl.pallas_call(functools.partial(scatter_kernel, axes), out_shape=pltpu.V...  39.6 us
    pallas_call x1, Pallas kernels, gather(): call(shifts, own, measured, probe, *tables, *sorted_by_residue(side_len))  38.8 us
    pallas_call x1, Pallas kernels, solve(): pl.pallas_call(solve_kernel, out_shape=pltpu.VMEM(grown.shape, grown.dtyp...  13.3 us
    unnamed x1, local copies, waits for them, and re-layouts  2.19 us

profile of v2, /device:TPU:8, one launch (start us, length us, event | category | flops | bytes accessed | tf_op | source)
XLA Modules:
  0.0 93.9 jit_solution(4989166889785167715)
XLA Ops:
  0.0 38.8 %shard_map.91 = (bf16[2,10,1280,128]{3,2,1,0:T(8,128)(2,1)S(1)}, f32[6,2,4,512,128]{4,3,2,1,0:T(8,128)S(1)}, bf16[6,2,2,4,2,256,128]{6,5,4,3,2,1,0:T(8,128)(2,1)...) custom-call(s32[2,6]{1,0:T(2,128)} %bitcast.6, f32[2,768,768]{2,1,0:T(8,128)} %own_hbm.1, ...), custom_call_target="tpu_custom_call" | custom-call | tf_op jit(solution)/shard_map/pallas_call | solution.py:401
  38.8 13.3 %shard_map.92.grown = f32[2,10,1280,128]{3,2,1,0:T(8,128)S(1)} custom-call(s32[1,8]{1,0:T(1,128)} %bitcast.8, s32[2,6]{1,0:T(2,128)} %bitcast.7, bf16[2,10,1280,128]{3,2,1,0:T(8,128)(2,1)S(1)} %get-tuple-element.10.field, f32[6,2,4,512,128]{4,3,2,1,0:T(8,128)S(1)} %get-tuple-element.11.probes, ...), custom_call_target="tpu_custom_call", output_to_operand_aliasing={{}: (6, {})} | custom-call | tf_op jit(solution)/shard_map/pallas_call | solution.py:688
  52.1 39.6 %shard_map.93 = f32[2,768,768]{2,1,0:T(8,128)S(1)} custom-call(f32[2,10,1280,128]{3,2,1,0:T(8,128)S(1)} %shard_map.92.grown), custom_call_target="tpu_custom_call" | custom-call | tf_op jit(solution)/shard_map/pallas_call | solution.py:522
  91.7 2.2 %copy.13 = f32[2,768,768]{2,1,0:T(8,128)} copy(f32[2,768,768]{2,1,0:T(8,128)S(1)} %shard_map.93) | data formatting | bytes 9437184
